TPU v7x, 256 devices: a whole 4x4x8 slice. The times are simulated.
256 devices in a mesh: blk: 32 (over z, y_hi, core), cls: 8 (over x, y_lo).
Axes of the slice: x: 4, y: 4 (y_hi: 2, y_lo: 2; y = y_hi * 2 + y_lo), z: 8, core: 2. Of those that a mesh axis runs over, the one named last changes fastest.
Arguments:
- features: bfloat16 [2048, 2048], P('blk'), may hold values from -6 to 6
- labels: int32 [2048], P('blk'), may hold values from 0 to 655359
- offset: int32 [1], replicated, may hold values from 0 to 524288
- other_lse: float32 [2048], replicated, may hold values from 15 to 20
- weight: bfloat16 [131072, 2048], P(('blk', 'cls'))
- accum: float32 [131072, 2048], P(('blk', 'cls')), may hold values from 0.1 to 1
Outputs:
- new_weight: bfloat16 [131072, 2048], P(('blk', 'cls'))
- new_accum: float32 [131072, 2048], P(('blk', 'cls'))
- lse: float32 [2048], P('blk')
All inputs are finite; a program needn't handle non-finite values.
Results may differ from a plain program's by a relative error of at most 0.004.
Values may be sent and summed in bfloat16 or wider, within the bound.
A program may use at most 128 MiB of HBM per device.

v0:
```python
import jax
import jax.numpy as jnp
from jax import lax
from jax.sharding import PartitionSpec as P


def scores(rows, weight):
    return lax.dot_general(
        rows, weight, (((1,), (1,)), ((), ())), preferred_element_type=jnp.float32
    )


def gradient_term(logits, lse_rows, label_rows, first_class, rows):
    width = logits.shape[1]
    local = label_rows - first_class
    onehot = (local[:, None] == jnp.arange(width, dtype=jnp.int32)[None, :]).astype(jnp.float32)
    delta = (jnp.exp(logits - lse_rows[:, None]) - onehot).astype(jnp.bfloat16)
    return lax.dot_general(
        delta, rows, (((0,), (0,)), ((), ())), preferred_element_type=jnp.float32
    )


def body(features, labels, offset, other_lse, weight, accum):
    block = features.shape[0]
    cls_dev = weight.shape[0]
    device_rank = lax.axis_index("blk") * lax.axis_size("cls") + lax.axis_index("cls")
    first_class = offset[0] + device_rank * cls_dev
    all_rows, all_labels = (
        lax.all_gather(features, "blk", axis=0, tiled=True),
        lax.all_gather(labels, "blk", axis=0, tiled=True),
    )
    logits = scores(all_rows, weight)
    local_top = jnp.max(logits, axis=1)
    top = lax.pmax(local_top, ("blk", "cls"))
    total = lax.psum(jnp.sum(jnp.exp(logits - top[:, None]), axis=1), ("blk", "cls"))
    slab_lse = top + jnp.log(total)
    high = jnp.maximum(slab_lse, other_lse)
    lse = high + jnp.log(jnp.exp(slab_lse - high) + jnp.exp(other_lse - high))
    grad = gradient_term(logits, lse, all_labels, first_class, all_rows)
    new_accum = accum + grad * grad
    new_weight = (weight.astype(jnp.float32) - 0.05 * grad / (jnp.sqrt(new_accum) + 1e-10)).astype(
        jnp.bfloat16
    )
    own_lse = lax.dynamic_slice_in_dim(lse, lax.axis_index("blk") * block, block, 0)
    return (new_weight, new_accum, own_lse)


def solution(mesh):
    in_specs = (
        P("blk", None),
        P("blk"),
        P(),
        P(),
        P(("blk", "cls"), None),
        P(("blk", "cls"), None),
    )
    out_specs = (P(("blk", "cls"), None), P(("blk", "cls"), None), P("blk"))
    return jax.shard_map(body, mesh=mesh, in_specs=in_specs, out_specs=out_specs, check_vma=False)
```

profile of v0, /device:TPU:1, one launch (start us, length us, event | category | flops | bytes accessed | tf_op | source)
XLA Modules:
  0.0 299.9 jit_solution(17665709030679258281)
XLA Ops:
  7.2 0.0 all-gather.2.cloned.1.call-start
  7.2 0.7 all-gather.2.cloned.1.call-update
  8.6 1.3 dynamic-slice
  10.5 0.9 dynamic-update-slice
  11.4 18.9 %all-reduce = s32[2048]{0:T(1024)S(1)} all-reduce(s32[2048]{0:T(1024)S(1)} %dynamic-update-slice), channel_id=1, replica_groups=mesh['blk'=32,'cls'=8] {'blk'}, use_global_device_ids=true, to_apply=%add | all-reduce | flops 2048 | bytes 16384
  30.2 86.2 %all-gather.2.cloned.1.call-done = bf16[2048,2048]{1,0:T(8,128)(2,1)} async-done(((bf16[64,2048]{1,0:T(8,128)(2,1)}), bf16[2048,2048]{1,0:T(8,128)(2,1)}) %all-gather.2.cloned.1.call-update) | async-done | bytes 8388624 | tf_op jit(solution)/shard_map/all_gather | solution.py:29
  116.5 10.5 %fusion.4 = (f32[2048]{0:T(1024)S(1)}, f32[2048,512]{0,1:T(8,128)}) fusion(bf16[2048,2048]{1,0:T(8,128)(2,1)} %all-gather.2.cloned.1.call-done, bf16[512,2048]{1,0:T(8,128)(2,1)} %param.10), kind=kOutput, calls=%fused_computation.12 | convolution fusion | flops 4296013824 | bytes 14688256 | tf_op jit(solution)/shard_map/dot_general | solution.py:8
  127.0 0.0 copy-start
  127.0 0.0 copy-start.1
  127.0 74.8 %pmax.7 = f32[2048]{0:T(1024)S(1)} all-reduce(f32[2048]{0:T(1024)S(1)} %get-tuple-element.5), channel_id=1, replica_groups=mesh['blk'=32,'cls'=8] {'blk','cls'}, use_global_device_ids=true, to_apply=%region_1.0 | all-reduce | flops 2048 | bytes 16384 | tf_op jit(solution)/shard_map/pmax | solution.py:34
  201.8 2.8 exponential_reduce_fusion
  204.5 73.3 %psum.7 = f32[2048]{0:T(1024)S(1)} all-reduce(f32[2048]{0:T(1024)S(1)} %exponential_reduce_fusion), channel_id=1, replica_groups=mesh['blk'=32,'cls'=8] {'blk','cls'}, use_global_device_ids=true, to_apply=%region_3.0 | all-reduce | flops 2048 | bytes 16384 | tf_op jit(solution)/shard_map/psum | solution.py:35
  277.8 0.0 copy-done
  277.9 0.6 dynamic_slice.3
  278.5 0.0 copy-done.1
  278.5 14.6 %subtract_convert_fusion = (bf16[512,2048]{1,0:T(8,128)(2,1)}, f32[512,2048]{1,0:T(8,128)}) fusion(bf16[512,2048]{1,0:T(8,128)(2,1)S(1)} %copy-done.1, f32[512,2048]{1,0:T(8,128)} %param.11, bf16[2048,2048]{1,0:T(8,128)(2,1)} %all-gather.2.cloned.1.call-done, f32[2048,512]{0,1:T(8,128)} %get-tuple-element.6, s32[2048]{0:T(1024)S(1)} %broadcast_subtract_fusion, ...), kind=kOutput, calls=%fused_computation | convolution fusion | flops 4308598784 | bytes 25182208 | tf_op jit(solution)/shard_map/dot_general | solution.py:18
  (3 shorter events, 0.0 us)
Async XLA Ops:
  7.2 109.3 %all-gather.2.cloned.1.call-start = ((), (), s32[]{:S(2)}) async-start(), calls=%async_computation | async-start | bytes 8650752 | tf_op jit(solution)/shard_map/all_gather | solution.py:29
  127.0 150.9 %copy-start = (f32[2048]{0:T(1024)S(1)}, f32[2048]{0:T(1024)}, u32[]{:S(2)}) copy-start(f32[2048]{0:T(1024)} %param.9) | copy-start | bytes 24580
  127.0 151.5 %copy-start.1 = (bf16[512,2048]{1,0:T(8,128)(2,1)S(1)}, bf16[512,2048]{1,0:T(8,128)(2,1)}, u32[]{:S(2)}) copy-start(bf16[512,2048]{1,0:T(8,128)(2,1)} %param.10) | copy-start | bytes 6291460
Sparse Core Ops, SparseCore 0:
  10.8 105.6 all-gather.1
where the time goes:
time: 300 us
  blocking collectives  167 us (56%)
  waiting for transfers between devices  86.9 us (29%)
  matrix products  25.1 us (8%)
  between operations  15.4 us (5%)
    all_gather x1, waiting for transfers between devices, body(): lax.all_gather(features, 'blk', axis=0, tiled=True)  86.2 us
    pmax x1, blocking collectives, body(): top = lax.pmax(local_top, ('blk', 'cls'))  74.8 us
    psum x1, blocking collectives, body(): lax.psum(jnp.sum(jnp.exp(logits - top[:, None]), axis=1), ('blk', 'cls'))  73.3 us
    unnamed x1, blocking collectives  18.9 us
    dot_general x1, matrix products, gradient_term(): lax.dot_general(delta, rows, (((0,), (0,)), ((), ())), preferred_element_...  14.6 us
    dot_general x1, matrix products, scores(): lax.dot_general(rows, weight, (((1,), (1,)), ((), ())), preferred_element...  10.5 us
  transfers between devices with their start and end apart: 1, of which 1 were waited for; matrix products, arithmetic and copies ran while one was open for 1% of the time, Pallas kernels for 0%

commit v1 on v0

--- a/solution.py
+++ b/solution.py
@@ -2,6 +2,11 @@
 import jax.numpy as jnp
 from jax import lax
 from jax.sharding import PartitionSpec as P
+
+
+def summed_here(shard, mesh_axis):
+    parts = lax.all_gather(shard, mesh_axis)
+    return jnp.sum(parts, axis=0)
 
 
 def scores(rows, weight):
@@ -32,7 +37,7 @@
     logits = scores(all_rows, weight)
     local_top = jnp.max(logits, axis=1)
     top = lax.pmax(local_top, ("blk", "cls"))
-    total = lax.psum(jnp.sum(jnp.exp(logits - top[:, None]), axis=1), ("blk", "cls"))
+    total = summed_here(jnp.sum(jnp.exp(logits - top[:, None]), axis=1), ("blk", "cls"))
     slab_lse = top + jnp.log(total)
     high = jnp.maximum(slab_lse, other_lse)
     lse = high + jnp.log(jnp.exp(slab_lse - high) + jnp.exp(other_lse - high))

time: 300 us -> 923 us (3.08)
  waiting for transfers between devices: 86.9 us -> 786 us
  blocking collectives: 167 us -> 86.8 us
    all_gather x0 -> x1, waiting for transfers between devices: none -> 677 us  [summed_here(): parts = lax.all_gather(shard, mesh_axis)]
    psum x1 -> x0, blocking collectives: 73.3 us -> none  [body(): lax.psum(jnp.sum(jnp.exp(logits - top[:, None]), axis=1), ('blk', 'cls'))]
    all_gather x1, waiting for transfers between devices: 86.2 us -> 109 us  [body(): lax.all_gather(features, 'blk', axis=0, tiled=True)]
  transfers between devices with their start and end apart: 1 -> 2, of which waited for: 1 -> 2; matrix products, arithmetic and copies ran while one was open for 1% -> 0% of each run, Pallas kernels for 0% -> 0%
where the time goes in v1:
time: 923 us; the launch traced here: 921 us
  waiting for transfers between devices  786 us (85%)
  blocking collectives  86.8 us (9%)
  matrix products  25.6 us (3%)
  between operations  15.4 us (2%)
    all_gather x1, waiting for transfers between devices, summed_here(): parts = lax.all_gather(shard, mesh_axis)  677 us
    all_gather x1, waiting for transfers between devices, body(): lax.all_gather(features, 'blk', axis=0, tiled=True)  109 us
    pmax x1, blocking collectives, body(): top = lax.pmax(local_top, ('blk', 'cls'))  74.8 us
  transfers between devices with their start and end apart: 2, of which 2 were waited for; matrix products, arithmetic and copies ran while one was open for 0% of the time, Pallas kernels for 0%

profile of v1, /device:TPU:1, one launch (start us, length us, event | category | flops | bytes accessed | tf_op | source)
XLA Modules:
  0.0 920.6 jit_solution(5326063140376025625)
XLA Ops:
  7.2 0.0 all-gather.4.cloned.1.call-start
  7.2 0.7 all-gather.4.cloned.1.call-update
  7.9 0.0 all-gather.6.cloned.1.call-start
  7.9 108.5 %all-gather.4.cloned.1.call-done = bf16[2048,2048]{1,0:T(8,128)(2,1)} async-done(((bf16[64,2048]{1,0:T(8,128)(2,1)}), bf16[2048,2048]{1,0:T(8,128)(2,1)}) %all-gather.4.cloned.1.call-update) | async-done | bytes 8388624 | tf_op jit(solution)/shard_map/all_gather | solution.py:34
  116.5 10.5 %fusion.4 = (f32[2048]{0:T(1024)S(1)}, f32[2048,512]{0,1:T(8,128)}) fusion(bf16[2048,2048]{1,0:T(8,128)(2,1)} %all-gather.4.cloned.1.call-done, bf16[512,2048]{1,0:T(8,128)(2,1)} %param.10), kind=kOutput, calls=%fused_computation.12 | convolution fusion | flops 4296013824 | bytes 14688256 | tf_op jit(solution)/shard_map/dot_general | solution.py:13
  127.0 0.0 copy-start.2
  127.0 0.0 copy-start.1
  127.0 74.8 %pmax.7 = f32[2048]{0:T(1024)S(1)} all-reduce(f32[2048]{0:T(1024)S(1)} %get-tuple-element.5), channel_id=1, replica_groups=mesh['blk'=32,'cls'=8] {'blk','cls'}, use_global_device_ids=true, to_apply=%region_1.0 | all-reduce | flops 2048 | bytes 16384 | tf_op jit(solution)/shard_map/pmax | solution.py:39
  201.7 3.4 exponential_reduce_fusion
  205.1 0.0 copy-start
  205.1 0.0 all-gather.6.cloned.1.call-update
  205.8 0.0 copy-done.2
  205.8 0.6 dynamic-slice
  207.1 0.0 copy-done.1
  207.1 0.3 dynamic-update-slice
  207.3 12.0 %all-reduce = s32[2048]{0:T(1024)S(1)} all-reduce(s32[2048]{0:T(1024)S(1)} %dynamic-update-slice), channel_id=1, replica_groups=mesh['blk'=32,'cls'=8] {'blk'}, use_global_device_ids=true, to_apply=%add | all-reduce | flops 2048 | bytes 16384
  219.4 676.7 %all-gather.6.cloned.1.call-done = f32[524288]{0:T(1024)} async-done(((f32[2048]{0:T(1024)}), f32[524288]{0:T(1024)}) %all-gather.6.cloned.1.call-update) | async-done | bytes 2097168 | tf_op jit(solution)/shard_map/all_gather | solution.py:8
  896.1 1.7 reshape.9
  897.9 0.1 reduce_sum.19
  898.0 0.0 copy-done
  898.0 0.6 dynamic_slice.3
  898.6 15.2 %subtract_convert_fusion = (bf16[512,2048]{1,0:T(8,128)(2,1)}, f32[512,2048]{1,0:T(8,128)}) fusion(bf16[512,2048]{1,0:T(8,128)(2,1)} %param.10, f32[512,2048]{1,0:T(8,128)} %param.11, bf16[2048,2048]{1,0:T(8,128)(2,1)} %all-gather.4.cloned.1.call-done, f32[2048,512]{0,1:T(8,128)} %get-tuple-element.6, s32[2048]{0:T(1024)S(1)} %broadcast_subtract_fusion, ...), kind=kOutput, calls=%fused_computation | convolution fusion | flops 4308598784 | bytes 25182208 | tf_op jit(solution)/shard_map/dot_general | solution.py:23
  (3 shorter events, 0.0 us)
Async XLA Ops:
  7.2 109.3 %all-gather.4.cloned.1.call-start = ((), (), s32[]{:S(2)}) async-start(), calls=%async_computation | async-start | bytes 8650752 | tf_op jit(solution)/shard_map/all_gather | solution.py:34
  7.9 888.3 %all-gather.6.cloned.1.call-start = ((), (), s32[]{:S(2)}) async-start(), calls=%async_computation.1 | async-start | bytes 2105344 | tf_op jit(solution)/shard_map/all_gather | solution.py:8
  127.0 78.8 %copy-start.2 = (u32[256]{0:T(256)S(1)}, u32[256]{0:T(256)}, u32[]{:S(2)}) copy-start(u32[256]{0:T(256)} %constant.29) | copy-start | bytes 3076
  127.0 80.1 %copy-start.1 = (s32[64]{0:T(128)S(1)}, s32[64]{0:T(128)}, u32[]{:S(2)}) copy-start(s32[64]{0:T(128)} %param.7) | copy-start | bytes 772
  205.1 692.9 %copy-start = (f32[2048]{0:T(1024)S(1)}, f32[2048]{0:T(1024)}, u32[]{:S(2)}) copy-start(f32[2048]{0:T(1024)} %param.9) | copy-start | bytes 24580
Sparse Core Ops, SparseCore 0:
  10.8 105.6 all-gather.3
  205.3 690.8 all-gather.5

commit v2 on v0

--- a/solution.py
+++ b/solution.py
@@ -21,6 +21,10 @@
 
 
 def body(features, labels, offset, other_lse, weight, accum):
+
+    def fix_body(xin):
+        return jax.lax.psum(jax.lax.psum(xin, axis_name="cls"), axis_name="blk")
+
     block = features.shape[0]
     cls_dev = weight.shape[0]
     device_rank = lax.axis_index("blk") * lax.axis_size("cls") + lax.axis_index("cls")
@@ -32,7 +36,7 @@
     logits = scores(all_rows, weight)
     local_top = jnp.max(logits, axis=1)
     top = lax.pmax(local_top, ("blk", "cls"))
-    total = lax.psum(jnp.sum(jnp.exp(logits - top[:, None]), axis=1), ("blk", "cls"))
+    total = fix_body(jnp.sum(jnp.exp(logits - top[:, None]), axis=1))
     slab_lse = top + jnp.log(total)
     high = jnp.maximum(slab_lse, other_lse)
     lse = high + jnp.log(jnp.exp(slab_lse - high) + jnp.exp(other_lse - high))

time: 300 us -> 311 us (1.037)
  blocking collectives: 167 us -> 177 us
    psum x1 -> x2, blocking collectives: 73.3 us -> 83.8 us  [fix_body(): return jax.lax.psum(jax.lax.psum(xin, axis_name='cls'), axis_name='blk')]
where the time goes in v2:
time: 311 us; the launch traced here: 310 us
  blocking collectives  177 us (57%)
  waiting for transfers between devices  86.9 us (28%)
  matrix products  25.1 us (8%)
  between operations  15.4 us (5%)
    all_gather x1, waiting for transfers between devices, body(): lax.all_gather(features, 'blk', axis=0, tiled=True)  86.2 us
    psum x2, blocking collectives, fix_body(): return jax.lax.psum(jax.lax.psum(xin, axis_name='cls'), axis_name='blk')  83.8 us
    pmax x1, blocking collectives, body(): top = lax.pmax(local_top, ('blk', 'cls'))  74.8 us
    unnamed x1, blocking collectives  18.9 us
    dot_general x1, matrix products, gradient_term(): lax.dot_general(delta, rows, (((0,), (0,)), ((), ())), preferred_element_...  14.6 us
    dot_general x1, matrix products, scores(): lax.dot_general(rows, weight, (((1,), (1,)), ((), ())), preferred_element...  10.5 us
  transfers between devices with their start and end apart: 1, of which 1 were waited for; matrix products, arithmetic and copies ran while one was open for 1% of the time, Pallas kernels for 0%

profile of v2, /device:TPU:1, one launch (start us, length us, event | category | flops | bytes accessed | tf_op | source)
XLA Modules:
  0.0 310.4 jit_solution(328261019161317494)
XLA Ops:
  7.2 0.0 all-gather.2.cloned.1.call-start
  7.2 0.7 all-gather.2.cloned.1.call-update
  8.6 1.3 dynamic-slice
  10.5 0.9 dynamic-update-slice
  11.4 18.9 %all-reduce = s32[2048]{0:T(1024)S(1)} all-reduce(s32[2048]{0:T(1024)S(1)} %dynamic-update-slice), channel_id=1, replica_groups=mesh['blk'=32,'cls'=8] {'blk'}, use_global_device_ids=true, to_apply=%add | all-reduce | flops 2048 | bytes 16384
  30.2 86.2 %all-gather.2.cloned.1.call-done = bf16[2048,2048]{1,0:T(8,128)(2,1)} async-done(((bf16[64,2048]{1,0:T(8,128)(2,1)}), bf16[2048,2048]{1,0:T(8,128)(2,1)}) %all-gather.2.cloned.1.call-update) | async-done | bytes 8388624 | tf_op jit(solution)/shard_map/all_gather | solution.py:33
  116.5 10.5 %fusion.4 = (f32[2048]{0:T(1024)S(1)}, f32[2048,512]{0,1:T(8,128)}) fusion(bf16[2048,2048]{1,0:T(8,128)(2,1)} %all-gather.2.cloned.1.call-done, bf16[512,2048]{1,0:T(8,128)(2,1)} %param.10), kind=kOutput, calls=%fused_computation.12 | convolution fusion | flops 4296013824 | bytes 14688256 | tf_op jit(solution)/shard_map/dot_general | solution.py:8
  127.0 0.0 copy-start
  127.0 0.0 copy-start.1
  127.0 74.8 %pmax.7 = f32[2048]{0:T(1024)S(1)} all-reduce(f32[2048]{0:T(1024)S(1)} %get-tuple-element.5), channel_id=1, replica_groups=mesh['blk'=32,'cls'=8] {'blk','cls'}, use_global_device_ids=true, to_apply=%region_1.0 | all-reduce | flops 2048 | bytes 16384 | tf_op jit(solution)/shard_map/pmax | solution.py:38
  201.8 2.8 exponential_reduce_fusion
  204.5 14.0 %psum.14 = f32[2048]{0:T(1024)S(1)} all-reduce(f32[2048]{0:T(1024)S(1)} %exponential_reduce_fusion), channel_id=1, replica_groups=mesh['blk'=32,'cls'=8] {'cls'}, use_global_device_ids=true, to_apply=%region_3.0 | all-reduce | flops 2048 | bytes 16384 | tf_op jit(solution)/shard_map/psum | solution.py:26
  218.5 69.8 %psum.15 = f32[2048]{0:T(1024)S(1)} all-reduce(f32[2048]{0:T(1024)S(1)} %psum.14), channel_id=1, replica_groups=mesh['blk'=32,'cls'=8] {'blk'}, use_global_device_ids=true, to_apply=%region_4.0 | all-reduce | flops 2048 | bytes 16384 | tf_op jit(solution)/shard_map/psum | solution.py:26
  288.3 0.0 copy-done
  288.4 0.6 dynamic_slice.3
  289.0 0.0 copy-done.1
  289.0 14.6 %subtract_convert_fusion = (bf16[512,2048]{1,0:T(8,128)(2,1)}, f32[512,2048]{1,0:T(8,128)}) fusion(bf16[512,2048]{1,0:T(8,128)(2,1)S(1)} %copy-done.1, f32[512,2048]{1,0:T(8,128)} %param.11, bf16[2048,2048]{1,0:T(8,128)(2,1)} %all-gather.2.cloned.1.call-done, f32[2048,512]{0,1:T(8,128)} %get-tuple-element.6, s32[2048]{0:T(1024)S(1)} %broadcast_subtract_fusion, ...), kind=kOutput, calls=%fused_computation | convolution fusion | flops 4308598784 | bytes 25182208 | tf_op jit(solution)/shard_map/dot_general | solution.py:18
  (3 shorter events, 0.0 us)
Async XLA Ops:
  7.2 109.3 %all-gather.2.cloned.1.call-start = ((), (), s32[]{:S(2)}) async-start(), calls=%async_computation | async-start | bytes 8650752 | tf_op jit(solution)/shard_map/all_gather | solution.py:33
  127.0 161.4 %copy-start = (f32[2048]{0:T(1024)S(1)}, f32[2048]{0:T(1024)}, u32[]{:S(2)}) copy-start(f32[2048]{0:T(1024)} %param.9) | copy-start | bytes 24580
  127.0 162.0 %copy-start.1 = (bf16[512,2048]{1,0:T(8,128)(2,1)S(1)}, bf16[512,2048]{1,0:T(8,128)(2,1)}, u32[]{:S(2)}) copy-start(bf16[512,2048]{1,0:T(8,128)(2,1)} %param.10) | copy-start | bytes 6291460
Sparse Core Ops, SparseCore 0:
  10.8 105.6 all-gather.1

commit v3 on v0

--- a/solution.py
+++ b/solution.py
@@ -2,6 +2,12 @@
 import jax.numpy as jnp
 from jax import lax
 from jax.sharding import PartitionSpec as P
+
+
+def zones_group(arr):
+    shaped = jnp.stack([arr] * lax.psum(1, "blk"), 0)
+    arr_next = jnp.concatenate(lax.all_to_all(shaped, "blk", 0, 0), axis=0)
+    return arr_next
 
 
 def scores(rows, weight):
@@ -26,7 +32,7 @@
     device_rank = lax.axis_index("blk") * lax.axis_size("cls") + lax.axis_index("cls")
     first_class = offset[0] + device_rank * cls_dev
     all_rows, all_labels = (
-        lax.all_gather(features, "blk", axis=0, tiled=True),
+        zones_group(features),
         lax.all_gather(labels, "blk", axis=0, tiled=True),
     )
     logits = scores(all_rows, weight)

time: 300 us -> 386 us (1.29)
  blocking collectives: 167 us -> 337 us
  waiting for transfers between devices: 86.9 us -> 0.01 us
  between operations: 15.4 us -> 2.01 us
  starting transfers between devices: 0.04 us -> 12.9 us
  local copies, waits for them, and re-layouts: 2.74 us -> 6.69 us
    unnamed x1, blocking collectives: 18.9 us -> 185 us
    all_gather x1 -> x0, waiting for transfers between devices: 86.2 us -> none  [body(): lax.all_gather(features, 'blk', axis=0, tiled=True)]
    all_to_all x0 -> x1, starting transfers between devices: none -> 12.9 us  [zones_group(): arr_next = jnp.concatenate(lax.all_to_all(shaped, 'blk', 0, 0), axis=0)]
    another operation x0 -> x1, local copies, waits for them, and re-layouts: none -> 5.22 us  [zones_group(): shaped = jnp.stack([arr] * lax.psum(1, 'blk'), 0)]
  transfers between devices with their start and end apart: 1 -> 1, of which waited for: 1 -> 0; matrix products, arithmetic and copies ran while one was open for 1% -> 0% of each run, Pallas kernels for 0% -> 0%
where the time goes in v3:
time: 386 us; the launch traced here: 385 us
  blocking collectives  337 us (87%)
  matrix products  24 us (6%)
  starting transfers between devices  12.9 us (3%)
  local copies, waits for them, and re-layouts  6.69 us (2%)
    unnamed x1, blocking collectives  185 us
    pmax x1, blocking collectives, body(): top = lax.pmax(local_top, ('blk', 'cls'))  78.5 us
    psum x1, blocking collectives, body(): lax.psum(jnp.sum(jnp.exp(logits - top[:, None]), axis=1), ('blk', 'cls'))  73.4 us
    dot_general x1, matrix products, gradient_term(): lax.dot_general(delta, rows, (((0,), (0,)), ((), ())), preferred_element_...  14.6 us
    all_to_all x1, starting transfers between devices, zones_group(): arr_next = jnp.concatenate(lax.all_to_all(shaped, 'blk', 0, 0), axis=0)  12.9 us
    dot_general x1, matrix products, scores(): lax.dot_general(rows, weight, (((1,), (1,)), ((), ())), preferred_element...  9.45 us
  transfers between devices with their start and end apart: 1, of which 0 were waited for; matrix products, arithmetic and copies ran while one was open for 0% of the time, Pallas kernels for 0%

profile of v3, /device:TPU:1, one launch (start us, length us, event | category | flops | bytes accessed | tf_op | source)
XLA Modules:
  0.0 385.5 jit_solution(2320218505429204021)
XLA Ops:
  0.6 5.2 %stack.2 = bf16[32,64,2048]{2,1,0:T(8,128)(2,1)} broadcast(bf16[64,2048]{1,0:T(8,128)(2,1)} %param.6), dimensions={1,2} | broadcast | bytes 8650752 | tf_op jit(solution)/shard_map/stack | solution.py:8
  5.9 0.0 copy-start.3
  5.9 0.0 copy-start.2
  5.9 0.0 copy-start.1
  5.9 12.9 %all-to-all-start = ((bf16[32,64,2048]{2,1,0:T(8,128)(2,1)}), bf16[32,64,2048]{2,1,0:T(8,128)(2,1)}, u32[]{:S(2)}, u32[]{:S(2)}) async-start(bf16[32,64,2048]{2,1,0:T(8,128)(2,1)} %stack.2), calls=%async_computation | async-start | bytes 16777216 | tf_op jit(solution)/shard_map/all_to_all | solution.py:9
  19.5 0.0 copy-done.3
  19.5 0.6 dynamic-slice
  20.7 0.0 copy-done.2
  20.7 0.3 dynamic-update-slice
  21.0 185.1 %all-reduce = s32[2048]{0:T(1024)S(1)} all-reduce(s32[2048]{0:T(1024)S(1)} %dynamic-update-slice), channel_id=1, replica_groups=mesh['blk'=32,'cls'=8] {'blk'}, use_global_device_ids=true, to_apply=%add | all-reduce | flops 2048 | bytes 16384
  206.1 0.0 all-to-all-done
  206.1 0.0 copy-done.1
  206.1 9.5 %fusion.4 = (f32[2048]{0:T(1024)S(1)}, f32[2048,512]{0,1:T(8,128)}) fusion(bf16[2048,2048]{1,0:T(8,128)(2,1)} %bitcast, bf16[512,2048]{1,0:T(8,128)(2,1)S(1)} %copy-done.1), kind=kOutput, calls=%fused_computation.12 | convolution fusion | flops 4296013824 | bytes 14688256 | tf_op jit(solution)/shard_map/dot_general | solution.py:14
  215.6 0.0 copy-start
  215.6 78.5 %pmax.7 = f32[2048]{0:T(1024)S(1)} all-reduce(f32[2048]{0:T(1024)S(1)} %get-tuple-element.5), channel_id=1, replica_groups=mesh['blk'=32,'cls'=8] {'blk','cls'}, use_global_device_ids=true, to_apply=%region_1.0 | all-reduce | flops 2048 | bytes 16384 | tf_op jit(solution)/shard_map/pmax | solution.py:40
  294.1 2.8 exponential_reduce_fusion
  296.9 73.4 %psum.7 = f32[2048]{0:T(1024)S(1)} all-reduce(f32[2048]{0:T(1024)S(1)} %exponential_reduce_fusion), channel_id=1, replica_groups=mesh['blk'=32,'cls'=8] {'blk','cls'}, use_global_device_ids=true, to_apply=%region_3.0 | all-reduce | flops 2048 | bytes 16384 | tf_op jit(solution)/shard_map/psum | solution.py:41
  370.3 0.0 copy-done
  370.3 0.6 dynamic_slice.3
  370.9 14.6 %subtract_convert_fusion = (bf16[512,2048]{1,0:T(8,128)(2,1)}, f32[512,2048]{1,0:T(8,128)}) fusion(bf16[512,2048]{1,0:T(8,128)(2,1)S(1)} %copy-done.1, f32[512,2048]{1,0:T(8,128)} %param.11, bf16[2048,2048]{1,0:T(8,128)(2,1)} %bitcast, f32[2048,512]{0,1:T(8,128)} %get-tuple-element.6, s32[2048]{0:T(1024)S(1)} %broadcast_subtract_fusion, f32[2048]{0:T(1024)S(1)} %log_add_fusion), kind=kOutput, calls=%fused_computation | convolution fusion | flops 4308598784 | bytes 25182208 | tf_op jit(solution)/shard_map/dot_general | solution.py:24
  (3 shorter events, 0.0 us)
Async XLA Ops:
  5.9 13.6 %copy-start.3 = (u32[256]{0:T(256)S(1)}, u32[256]{0:T(256)}, u32[]{:S(2)}) copy-start(u32[256]{0:T(256)} %constant.29) | copy-start | bytes 3076
  5.9 14.9 %copy-start.2 = (s32[64]{0:T(128)S(1)}, s32[64]{0:T(128)}, u32[]{:S(2)}) copy-start(s32[64]{0:T(128)} %param.7) | copy-start | bytes 772
  5.9 200.3 %copy-start.1 = (bf16[512,2048]{1,0:T(8,128)(2,1)S(1)}, bf16[512,2048]{1,0:T(8,128)(2,1)}, u32[]{:S(2)}) copy-start(bf16[512,2048]{1,0:T(8,128)(2,1)} %param.10) | copy-start | bytes 6291460
  5.9 200.3 %all-to-all-start = ((bf16[32,64,2048]{2,1,0:T(8,128)(2,1)}), bf16[32,64,2048]{2,1,0:T(8,128)(2,1)}, u32[]{:S(2)}, u32[]{:S(2)}) async-start(bf16[32,64,2048]{2,1,0:T(8,128)(2,1)} %stack.2), calls=%async_computation | async-start | bytes 16777216 | tf_op jit(solution)/shard_map/all_to_all | solution.py:9
  215.6 154.7 %copy-start = (f32[2048]{0:T(1024)S(1)}, f32[2048]{0:T(1024)}, u32[]{:S(2)}) copy-start(f32[2048]{0:T(1024)} %param.9) | copy-start | bytes 24580
